TPU v7x, 32 devices: a whole 2x2x4 slice. The times are simulated.
32 devices in a mesh: gx: 2 (over core), gy: 4 (over z), gz: 4 (over y, x).
Axes of the slice: x: 2, y: 2, z: 4, core: 2. Of those that a mesh axis runs over, the one named last changes fastest.
Arguments:
- head_old: float32 [256, 16, 512], P('gz', 'gx', 'gy'), may hold values from -0.5 to -0.05
- ks_scale: float32 [256, 16, 512], P('gz', 'gx', 'gy'), may hold values from 0.5 to 2
- soil_class: int32 [256, 16, 512], P('gz', 'gx', 'gy'), may hold values from 0 to 5
- emitter_cells: int32 [2, 4, 256], P('gx', 'gy'), may hold values from 0 to 1023
Outputs:
- head: float32 [256, 16, 512], P('gz', 'gx', 'gy')
- water: float32 [256, 16, 512], P('gz', 'gx', 'gy')
All inputs are finite; a program needn't handle non-finite values.
Results may differ from a plain program's by a relative error of at most 0.0003.
Values sent between devices are 32-bit elements; how exact they have to be, the bound alone decides.
No kernel may reach another device: no remote copies, remote signals or barrier semaphores. Data moves between devices by JAX's collectives and lax.ppermute only.
A program may use at most 64 MiB of HBM per device.

v0:
```python
import jax
import jax.numpy as jnp
from jax import lax
from jax.sharding import PartitionSpec as P

ITERS = 2
DRIP = 30


ALPHA_TABLE = (3.6, 2.0, 1.9, 1.0, 5.9, 1.6)
SHAPE_TABLE = (1.56, 1.41, 1.31, 1.23, 1.48, 1.37)
RESIDUAL_TABLE = (0.078, 0.067, 0.095, 0.089, 0.1, 0.034)
SATURATED_TABLE = (0.43, 0.45, 0.41, 0.43, 0.39, 0.46)
CONDUCT_TABLE = (0.2496, 0.108, 0.0624, 0.0168, 0.3144, 0.06)
layer_height = 0.01
column_width = 2.0
time_step = 2.0
storage_floor = 0.001
emitter_flow = 0.096
vertical_gain = 1.0 / (layer_height * layer_height)
gravity_gain = 1.0 / layer_height
lateral_gain = 1.0 / (column_width * column_width)
storage_gain = 1.0 / time_step
emitter_rate = emitter_flow / (column_width * column_width * layer_height)


def padded(value, sides, width):
    for axis, dim in sides:
        size, length = (lax.axis_size(axis), value.shape[dim])
        up = [(i, (i + 1) % size) for i in range(size - 1)]
        down = [(j, i) for i, j in up]
        last = lax.slice_in_dim(value, length - width, length, axis=dim)
        initial = lax.slice_in_dim(value, 0, width, axis=dim)
        before = lax.ppermute(last, axis, up)
        after = lax.ppermute(initial, axis, down)
        value = jnp.concatenate([before, value, after], axis=dim)
    return value


def carried_in(value, axis, join, neutral, backward):
    count, mine = (lax.axis_size(axis), lax.axis_index(axis))
    pieces = jax.tree.map(lambda part: lax.all_gather(part, axis), value)
    if backward:
        pieces = jax.tree.map(lambda part: part[::-1], pieces)
        mine = count - 1 - mine
    running = jax.tree.map(
        lambda part, zero: jnp.full_like(part, 0) + jnp.asarray(zero, part.dtype), value, neutral
    )

    def lap(position, running):
        longer = join(running, jax.tree.map(lambda part: part[position], pieces))
        return jax.tree.map(lambda new, old: jnp.where(position < mine, new, old), longer, running)

    return lax.fori_loop(0, count - 1, lap, running)


def soil_params(soil_class, ks_scale):
    air_entry = jnp.zeros(soil_class.shape, jnp.float32)
    shape_n = air_entry
    theta_res = air_entry
    theta_sat = air_entry
    sat_conduct = air_entry
    for number in range(len(ALPHA_TABLE)):
        chosen = soil_class == number
        air_entry = jnp.where(chosen, ALPHA_TABLE[number], air_entry)
        shape_n = jnp.where(chosen, SHAPE_TABLE[number], shape_n)
        theta_res = jnp.where(chosen, RESIDUAL_TABLE[number], theta_res)
        theta_sat = jnp.where(chosen, SATURATED_TABLE[number], theta_sat)
        sat_conduct = jnp.where(chosen, CONDUCT_TABLE[number], sat_conduct)
    return (air_entry, shape_n, theta_res, theta_sat, sat_conduct * ks_scale)


def effective_state(pressure, air_entry, shape_n):
    shape_m = 1.0 - 1.0 / shape_n
    scaled = air_entry * jnp.abs(pressure)
    lifted = 1.0 + scaled**shape_n
    effective = jnp.where(pressure < 0.0, lifted ** (-shape_m), 1.0)
    return (effective, scaled, lifted, shape_m)


def flow_factor(effective, shape_m, sat_conduct):
    inner_term = 1.0 - (1.0 - effective ** (1.0 / shape_m)) ** shape_m
    return sat_conduct * jnp.sqrt(effective) * inner_term * inner_term


def retention(pressure, air_entry, shape_n, theta_res, theta_sat, sat_conduct):
    effective, scaled, lifted, shape_m = effective_state(pressure, air_entry, shape_n)
    spread = theta_sat - theta_res
    moisture = theta_res + spread * effective
    capacity_core = jnp.where(
        pressure < 0.0,
        spread
        * air_entry
        * shape_n
        * shape_m
        * scaled ** (shape_n - 1.0)
        * lifted ** (-shape_m - 1.0),
        0.0,
    )
    return (moisture, flow_factor(effective, shape_m, sat_conduct), capacity_core + storage_floor)


def assemble(z_face, z_head, x_face, x_head, y_face, y_head, moisture, capacity, theta_old, source):
    z_flux = z_face * ((z_head[:-1] - z_head[1:]) * vertical_gain + gravity_gain)
    x_flux = x_face * (x_head[:, :-1] - x_head[:, 1:]) * lateral_gain
    y_flux = y_face * (y_head[:, :, :-1] - y_head[:, :, 1:]) * lateral_gain
    residual = (
        (moisture - theta_old) * storage_gain
        + (z_flux[1:] - z_flux[:-1])
        + (x_flux[:, 1:] - x_flux[:, :-1])
        + (y_flux[:, :, 1:] - y_flux[:, :, :-1])
        - source
    )
    z_gain = z_face * vertical_gain
    diagonal = (
        capacity * storage_gain
        + (z_gain[:-1] + z_gain[1:])
        + (x_face[:, 1:] + x_face[:, :-1]) * lateral_gain
        + (y_face[:, :, 1:] + y_face[:, :, :-1]) * lateral_gain
    )
    return (-z_gain[:-1], diagonal, -z_gain[1:], -residual)


def block_reduce(lower, diagonal, upper, right_side):
    first_a = lower[:2] / diagonal[:2]
    first_c = upper[:2] / diagonal[:2]
    first_d = right_side[:2] / diagonal[:2]

    def forward(carried, entries):
        a_prev, c_prev, d_prev = carried
        sub_entry, diag_entry, super_entry, rhs_entry = entries
        recip = 1.0 / (diag_entry - sub_entry * c_prev)
        d_new = recip * (rhs_entry - sub_entry * d_prev)
        a_new = -recip * sub_entry * a_prev
        c_new = recip * super_entry
        return ((a_new, c_new, d_new), (a_new, c_new, d_new))

    unused, (fwd_a, fwd_c, fwd_d) = lax.scan(
        forward,
        (first_a[1], first_c[1], first_d[1]),
        (lower[2:], diagonal[2:], upper[2:], right_side[2:]),
    )
    all_a = jnp.concatenate([first_a, fwd_a], axis=0)
    all_c = jnp.concatenate([first_c, fwd_c], axis=0)
    all_d = jnp.concatenate([first_d, fwd_d], axis=0)

    def backward(carried, entries):
        a_next, c_next, d_next = carried
        a_here, c_here, d_here = entries
        d_new = d_here - c_here * d_next
        a_new = a_here - c_here * a_next
        c_new = -c_here * c_next
        return ((a_new, c_new, d_new), (a_new, c_new, d_new))

    unused_b, (back_a, back_c, back_d) = lax.scan(
        backward,
        (all_a[-2], all_c[-2], all_d[-2]),
        (all_a[1:-2], all_c[1:-2], all_d[1:-2]),
        reverse=True,
    )
    mid_a = jnp.concatenate([back_a, all_a[-2:-1]], axis=0)
    mid_c = jnp.concatenate([back_c, all_c[-2:-1]], axis=0)
    mid_d = jnp.concatenate([back_d, all_d[-2:-1]], axis=0)
    recip_top = 1.0 / (1.0 - all_c[0] * mid_a[0])
    top_d = recip_top * (all_d[0] - all_c[0] * mid_d[0])
    top_a = recip_top * all_a[0]
    top_c = -recip_top * all_c[0] * mid_c[0]
    return ((top_a, top_c, top_d), (all_a[-1], all_c[-1], all_d[-1]), (mid_a, mid_c, mid_d))


def row_map(sub_entry, super_entry, rhs_entry):
    zeros_plane = jnp.zeros_like(sub_entry)
    ones_plane = jnp.ones_like(sub_entry)
    return jnp.stack(
        [
            jnp.stack([zeros_plane, zeros_plane, super_entry]),
            jnp.stack([zeros_plane, -sub_entry, rhs_entry]),
            jnp.stack([-sub_entry, zeros_plane, ones_plane]),
        ]
    )


def compose(left_map, right_map):
    product = jnp.sum(left_map[:, :, None] * right_map[None, :, :], axis=1)
    return product / jnp.max(jnp.abs(product), axis=(0, 1))


def forward_combine(earlier, later):
    return compose(later, earlier)


def apply_map(matrix, vector):
    return jnp.sum(matrix * vector[None], axis=1)


def backward_combine(earlier, later):
    return (later[0] * earlier[0], later[1] + later[0] * earlier[1])


def per_device(head_old, ks_scale, soil_class, emitter_cells):
    air_entry, shape_n, theta_res, theta_sat, sat_conduct = soil_params(soil_class, ks_scale)
    theta_old, unused_k, unused_c = retention(
        head_old, air_entry, shape_n, theta_res, theta_sat, sat_conduct
    )
    top_edge = lax.axis_index("gz") == 0
    bottom_edge = lax.axis_index("gz") == lax.axis_size("gz") - 1
    west_edge = lax.axis_index("gx") == 0
    east_edge = lax.axis_index("gx") == lax.axis_size("gx") - 1
    south_edge = lax.axis_index("gy") == 0
    north_edge = lax.axis_index("gy") == lax.axis_size("gy") - 1
    layer_count, row_count, col_count = head_old.shape
    emitter_spot = emitter_cells.reshape(-1)
    plane = (
        jnp.zeros((row_count, col_count), jnp.float32)
        .at[emitter_spot // col_count, emitter_spot % col_count]
        .add(emitter_rate)
    )
    plane = jnp.where(top_edge, plane, 0.0)
    source = jnp.zeros((layer_count, row_count, col_count), jnp.float32).at[DRIP].set(plane)
    pressure = head_old
    for iteration in range(ITERS):
        moisture, conductivity, capacity = retention(
            pressure, air_entry, shape_n, theta_res, theta_sat, sat_conduct
        )
        both_pad = padded(jnp.stack([pressure, conductivity]), (("gx", 2), ("gy", 3), ("gz", 1)), 1)
        head_pad = both_pad[0]
        cond_pad = both_pad[1]
        k_line = cond_pad[:, 1:-1, 1:-1]
        inner_z = 0.5 * (k_line[:-1] + k_line[1:])
        z_face = jnp.concatenate(
            [
                jnp.where(top_edge, 0.0, inner_z[:1]),
                inner_z[1:-1],
                jnp.where(bottom_edge, conductivity[-1:], inner_z[-1:]),
            ],
            axis=0,
        )
        k_rows = cond_pad[1:-1, :, 1:-1]
        inner_x = 0.5 * (k_rows[:, :-1] + k_rows[:, 1:])
        x_face = jnp.concatenate(
            [
                jnp.where(west_edge, 0.0, inner_x[:, :1]),
                inner_x[:, 1:-1],
                jnp.where(east_edge, 0.0, inner_x[:, -1:]),
            ],
            axis=1,
        )
        k_cols = cond_pad[1:-1, 1:-1, :]
        inner_y = 0.5 * (k_cols[:, :, :-1] + k_cols[:, :, 1:])
        y_face = jnp.concatenate(
            [
                jnp.where(south_edge, 0.0, inner_y[:, :, :1]),
                inner_y[:, :, 1:-1],
                jnp.where(north_edge, 0.0, inner_y[:, :, -1:]),
            ],
            axis=2,
        )
        lower, diagonal, upper, right_side = assemble(
            z_face,
            head_pad[:, 1:-1, 1:-1],
            x_face,
            head_pad[1:-1, :, 1:-1],
            y_face,
            head_pad[1:-1, 1:-1, :],
            moisture,
            capacity,
            theta_old,
            source,
        )
        (top_a, top_c, top_d), (last_a, last_c, last_d), (mid_a, mid_c, mid_d) = block_reduce(
            lower, diagonal, upper, right_side
        )
        map_top = row_map(top_a, top_c, top_d)
        map_last = row_map(last_a, last_c, last_d)
        block_map = compose(map_last, map_top)
        identity = jnp.broadcast_to(
            jnp.eye(3, dtype=jnp.float32)[:, :, None, None], block_map.shape
        )
        prefix = carried_in(block_map, "gz", forward_combine, identity, False)
        state_top = apply_map(map_top, prefix[:, 2])
        ratio_top = state_top[0] / state_top[2]
        shift_top = state_top[1] / state_top[2]
        state_last = apply_map(map_last, state_top)
        ratio_last = state_last[0] / state_last[2]
        shift_last = state_last[1] / state_last[2]
        tail = carried_in(
            (ratio_top * ratio_last, shift_top - ratio_top * shift_last),
            "gz",
            backward_combine,
            (jnp.ones_like(top_a), jnp.zeros_like(top_a)),
            True,
        )
        last_value = shift_last - ratio_last * tail[1]
        first_value = shift_top - ratio_top * last_value
        interior = mid_d - mid_a * first_value - mid_c * last_value
        correction = jnp.concatenate([first_value[None], interior, last_value[None]], axis=0)
        pressure = pressure + correction
    water, unused_k2, unused_c2 = retention(
        pressure, air_entry, shape_n, theta_res, theta_sat, sat_conduct
    )
    return (pressure, water)


def solution(mesh):
    in_specs = (P("gz", "gx", "gy"), P("gz", "gx", "gy"), P("gz", "gx", "gy"), P("gx", "gy", None))
    out_specs = (P("gz", "gx", "gy"), P("gz", "gx", "gy"))
    return jax.shard_map(
        per_device, mesh=mesh, in_specs=in_specs, out_specs=out_specs, check_vma=False
    )
```

profile of v0, /device:TPU:0, one launch (start us, length us, event | category | flops | bytes accessed | tf_op | source)
XLA Modules:
  0.0 147.9 jit_solution(11345833688656144057)
XLA Ops:
  0.6 3.3 %multiply_multiply_fusion.1 = (f32[64,8,128]{2,1,0:T(8,128)S(1)}, pred[64,8,128]{2,1,0:T(8,128)(4,1)S(1)}, pred[64,8,128]{2,1,0:T(8,128)(4,1)S(1)}, pred[64,8,12...) fusion(f32[64,8,128]{2,1,0:T(8,128)} %param.23, ...), kind=kLoop, calls=%fused_computation.86 | loop fusion | flops 2555904 | bytes 1441792 | tf_op jit(solution)/shard_map/mul | solution.py:83
  5.1 2.4 %collective-permute-start = (f32[2,64,1,128]{3,2,1,0:T(1,128)S(1)}, f32[2,64,1,128]{3,2,1,0:T(1,128)S(1)}, u32[]{:S(2)}, u32[]{:S(2)}) collective-permute-start(f32[2,64,1,128]{3,2,1,0:T(1,128)S(1)} %get-tuple-element.1125), channel_id=1, source_target_pairs={{0,16},{1,17},{2,18},{3,19},{4,20},{5,21},{6,22},{7,23},{8,24},{9,... | collective-permute-start | bytes 196616 | tf_op jit(solution)/shard_map/ppermute | solution.py:34
  9.5 11.2 %scatter_fusion = f32[8,128]{1,0:T(8,128)S(1)} fusion(f32[8,128]{1,0:T(8,128)S(1)} %broadcast.255, s32[256]{0:T(256)S(1)} %bitcast.278, f32[256]{0:T(256)S(1)} %broadcast.276), kind=kCustom, calls=%fused_computation | custom fusion | flops 256 | bytes 5120 | tf_op jit(solution)/shard_map/scatter-add | solution.py:216
  21.7 4.3 %collective-permute-start.2 = (f32[2,64,10,1]{1,0,3,2:T(2,128)S(1)}, f32[2,64,10,1]{1,0,3,2:T(2,128)S(1)}, u32[]{:S(2)}, u32[]{:S(2)}) collective-permute-start(f32[2,64,10,1]{1,0,3,2:T(2,128)S(1)} %copy.14), channel_id=1, source_target_pairs={{0,4},{4,8},{8,12},{1,5},{5,9},{9,13},{2,6},{6,10},{10,14},{3,7},{... | collective-permute-start | bytes 15368 | tf_op jit(solution)/shard_map/ppermute | solution.py:34
  28.3 3.7 %collective-permute-done.3 = f32[2,64,10,1]{1,0,3,2:T(2,128)S(1)} collective-permute-done((f32[2,64,10,1]{1,0,3,2:T(2,128)S(1)}, f32[2,64,10,1]{1,0,3,2:T(2,128)S(1)}, u32[]{:S(2)}, u32[]{:S(2)}) %collective-permute-start.3) | collective-permute-done | bytes 5152 | tf_op jit(solution)/shard_map/ppermute | solution.py:35
  32.6 3.4 %collective-permute-start.4 = (f32[2,1,10,130]{3,2,1,0:T(8,128)S(1)}, f32[2,1,10,130]{3,2,1,0:T(8,128)S(1)}, u32[]{:S(2)}, u32[]{:S(2)}) collective-permute-start(f32[2,1,10,130]{3,2,1,0:T(8,128)S(1)} %get-tuple-element.1105), channel_id=1, source_target_pairs={{0,1},{1,2},{2,3},{4,5},{5,6},{6,7},{8,9},{9,10},{10,11},{12,13},{... | collective-permute-start | bytes 31208 | tf_op jit(solution)/shard_map/ppermute | solution.py:34
  36.0 1.5 collective-permute-start.5
  37.6 4.2 %collective-permute-done.5 = f32[2,1,10,130]{3,2,1,0:T(8,128)S(1)} collective-permute-done((f32[2,1,10,130]{3,2,1,0:T(8,128)S(1)}, f32[2,1,10,130]{3,2,1,0:T(8,128)S(1)}, u32[]{:S(2)}, u32[]{:S(2)}) %collective-permute-start.5) | collective-permute-done | bytes 10432 | tf_op jit(solution)/shard_map/ppermute | solution.py:35
  41.8 1.4 pad_maximum_fusion
  45.5 2.1 %slice_negate_fusion.3 = (f32[64,8,128]{2,1,0:T(8,128)S(1)}, f32[64,8,128]{2,1,0:T(8,128)S(1)}, f32[64,8,128]{2,1,0:T(8,128)S(1)}) fusion(f32[65,8,128]{2,1,0:T(8,128)S(1)} %get-tuple-element.1135, f32[64,8,127]{2,1,0:T(8,128)S(1)} %slice.682, f32[64,8,1]{2,1,0:T(8,128)S(1)} %get-tuple-element.1121, f32[64,8,1]{2,1,0:T(8,128)S(1)} %get-tuple-element.1122, ...), kind=kLoop, calls=%fused_computation.167 | loop fusion | flops 3670016 | bytes 2525184 | tf_op jit(solution)/shard_map/neg | solution.py:121
  47.7 1.4 fusion.36
  49.2 3.7 %while.143 = (s32[]{:T(128)}, f32[8,128]{1,0:T(8,128)S(1)}, f32[8,128]{1,0:T(8,128)S(1)}, f32[8,128]{1,0:T(8,128)S(1)}, f32[62,8,128]{2,1,0:T(8,128)S(1)}, /*ind...) while((s32[]{:T(128)}, f32[8,128]{1,0:T(8,128)S(1)}, ...), condition=%wide.region_2.3_spmd, body=%wide.region_1.2_spmd.sunk | while | flops 10242 | bytes 65661 | solution.py:138
  53.1 2.3 %while.144 = (s32[]{:T(128)}, f32[8,128]{1,0:T(8,128)S(1)}, f32[8,128]{1,0:T(8,128)S(1)}, f32[8,128]{1,0:T(8,128)S(1)}, f32[61,8,128]{2,1,0:T(8,128)S(1)}, /*ind...) while((s32[]{:T(128)}, f32[8,128]{1,0:T(8,128)S(1)}, ...), condition=%wide.region_4.5_spmd, body=%wide.region_3.4_spmd.sunk | while | flops 6147 | bytes 49285 | solution.py:155
  55.6 9.5 %all_gather.24 = f32[4,3,3,8,128]{4,3,2,1,0:T(8,128)S(1)} all-gather(f32[1,3,3,8,128]{4,3,2,1,0:T(8,128)S(1)} %bitcast_divide_fusion.1), channel_id=1, replica_groups=mesh['gx'=2,'gy'=4,'gz'=4] {'gz'}, dimensions={0}, use_global_device_ids=true | all-gather | bytes 184320 | tf_op jit(solution)/shard_map/all_gather | solution.py:42
  65.4 6.7 %all_gather.25 = f32[4,8,128]{2,1,0:T(8,128)S(1)} all-gather(f32[1,8,128]{2,1,0:T(8,128)S(1)} %get-tuple-element.1174), channel_id=1, replica_groups=mesh['gx'=2,'gy'=4,'gz'=4] {'gz'}, dimensions={0}, use_global_device_ids=true | all-gather | bytes 20480 | tf_op jit(solution)/shard_map/all_gather | solution.py:42
  72.1 8.7 %all_gather.26 = f32[4,8,128]{2,1,0:T(8,128)S(1)} all-gather(f32[1,8,128]{2,1,0:T(8,128)S(1)} %get-tuple-element.1173), channel_id=1, replica_groups=mesh['gx'=2,'gy'=4,'gz'=4] {'gz'}, dimensions={0}, use_global_device_ids=true | all-gather | bytes 20480 | tf_op jit(solution)/shard_map/all_gather | solution.py:42
  81.0 2.1 %multiply_multiply_fusion = (f32[64,8,128]{2,1,0:T(8,128)S(1)}, f32[64,8,128]{2,1,0:T(8,128)S(1)}) fusion(f32[64,8,128]{2,1,0:T(8,128)S(1)} %copy-done.1, pred[64,8,128]{2,1,0:T(8,128)(4,1)S(1)} %get-tuple-element.1090, pred[64,8,128]{2,1,0:T(8,128)(4,1)S(1)} %get-tuple-element.1089, pred[64,8,128]{2,1,0:T(8,128)(4,1)S(1)} %get-tuple-element.1088, ...), kind=kLoop, calls=%fused_computation.85 | loop fusion | flops 2359296 | bytes 1703936 | tf_op jit(solution)/shard_map/mul | solution.py:83
  85.7 1.8 %collective-permute-done.7 = f32[2,64,1,128]{3,2,1,0:T(1,128)S(1)} collective-permute-done((f32[2,64,1,128]{3,2,1,0:T(1,128)S(1)}, f32[2,64,1,128]{3,2,1,0:T(1,128)S(1)}, u32[]{:S(2)}, u32[]{:S(2)}) %collective-permute-start.7) | collective-permute-done | bytes 65568 | tf_op jit(solution)/shard_map/ppermute | solution.py:35
  88.5 3.5 %collective-permute-start.8 = (f32[2,64,10,1]{1,0,3,2:T(2,128)S(1)}, f32[2,64,10,1]{1,0,3,2:T(2,128)S(1)}, u32[]{:S(2)}, u32[]{:S(2)}) collective-permute-start(f32[2,64,10,1]{1,0,3,2:T(2,128)S(1)} %copy.18), channel_id=1, source_target_pairs={{0,4},{4,8},{8,12},{1,5},{5,9},{9,13},{2,6},{6,10},{10,14},{3,7},{... | collective-permute-start | bytes 15368 | tf_op jit(solution)/shard_map/ppermute | solution.py:34
  92.3 1.5 %collective-permute-start.9 = (f32[2,64,10,1]{1,0,3,2:T(2,128)S(1)}, f32[2,64,10,1]{1,0,3,2:T(2,128)S(1)}, u32[]{:S(2)}, u32[]{:S(2)}) collective-permute-start(f32[2,64,10,1]{1,0,3,2:T(2,128)S(1)} %copy.19), channel_id=1, source_target_pairs={{4,0},{8,4},{12,8},{5,1},{9,5},{13,9},{6,2},{10,6},{14,10},{7,3},{... | collective-permute-start | bytes 15368 | tf_op jit(solution)/shard_map/ppermute | solution.py:35
  94.3 3.5 %collective-permute-done.9 = f32[2,64,10,1]{1,0,3,2:T(2,128)S(1)} collective-permute-done((f32[2,64,10,1]{1,0,3,2:T(2,128)S(1)}, f32[2,64,10,1]{1,0,3,2:T(2,128)S(1)}, u32[]{:S(2)}, u32[]{:S(2)}) %collective-permute-start.9) | collective-permute-done | bytes 5152 | tf_op jit(solution)/shard_map/ppermute | solution.py:35
  98.5 1.9 %collective-permute-start.10 = (f32[2,1,10,130]{3,2,1,0:T(8,128)S(1)}, f32[2,1,10,130]{3,2,1,0:T(8,128)S(1)}, u32[]{:S(2)}, u32[]{:S(2)}) collective-permute-start(f32[2,1,10,130]{3,2,1,0:T(8,128)S(1)} %get-tuple-element.1103), channel_id=1, source_target_pairs={{0,1},{1,2},{2,3},{4,5},{5,6},{6,7},{8,9},{9,10},{10,11},{12,13},{... | collective-permute-start | bytes 31208 | tf_op jit(solution)/shard_map/ppermute | solution.py:34
  102.0 4.2 %collective-permute-done.11 = f32[2,1,10,130]{3,2,1,0:T(8,128)S(1)} collective-permute-done((f32[2,1,10,130]{3,2,1,0:T(8,128)S(1)}, f32[2,1,10,130]{3,2,1,0:T(8,128)S(1)}, u32[]{:S(2)}, u32[]{:S(2)}) %collective-permute-start.11) | collective-permute-done | bytes 10432 | tf_op jit(solution)/shard_map/ppermute | solution.py:35
  106.2 1.4 pad_maximum_fusion.1
  109.9 2.1 %slice_negate_fusion.1 = (f32[64,8,128]{2,1,0:T(8,128)S(1)}, f32[64,8,128]{2,1,0:T(8,128)S(1)}, f32[64,8,128]{2,1,0:T(8,128)S(1)}) fusion(f32[65,8,128]{2,1,0:T(8,128)S(1)} %get-tuple-element.1128, f32[64,8,127]{2,1,0:T(8,128)S(1)} %slice.736, f32[64,8,1]{2,1,0:T(8,128)S(1)} %get-tuple-element.1115, f32[64,8,1]{2,1,0:T(8,128)S(1)} %get-tuple-element.1116, ...), kind=kLoop, calls=%fused_computation.165 | loop fusion | flops 3670016 | bytes 2525184 | tf_op jit(solution)/shard_map/neg | solution.py:121
  112.1 2.1 %fusion.37 = f32[64,8,128]{2,1,0:T(8,128)S(1)} fusion(f32[1,8,128]{2,1,0:T(8,128)S(1)} %select_bitcast_fusion, f32[64,8,129]{2,1,0:T(8,128)S(1)} %fusion.17, f32[64,9,128]{2,1,0:T(8,128)S(1)} %fusion.19, f32[65,8,128]{2,1,0:T(8,128)S(1)} %get-tuple-element.1127, pred[64,8,128]{2,1,0:T(8,128)(4,1)S(1)} %get-tuple-element.1090, ...), kind=kLoop, calls=%fused_computation.104 | loop fusion | flops 3407872 | bytes 2756608 | tf_op jit(solution)/shard_map/neg | solution.py:121
  114.4 3.6 %while.146 = (s32[]{:T(128)}, f32[8,128]{1,0:T(8,128)S(1)}, f32[8,128]{1,0:T(8,128)S(1)}, f32[8,128]{1,0:T(8,128)S(1)}, f32[62,8,128]{2,1,0:T(8,128)S(1)}, /*ind...) while((s32[]{:T(128)}, f32[8,128]{1,0:T(8,128)S(1)}, ...), condition=%wide.region_16.17_spmd, body=%wide.region_15.16_spmd.sunk | while | flops 10242 | bytes 65661 | solution.py:138
  118.2 2.3 %while.147 = (s32[]{:T(128)}, f32[8,128]{1,0:T(8,128)S(1)}, f32[8,128]{1,0:T(8,128)S(1)}, f32[8,128]{1,0:T(8,128)S(1)}, f32[61,8,128]{2,1,0:T(8,128)S(1)}, /*ind...) while((s32[]{:T(128)}, f32[8,128]{1,0:T(8,128)S(1)}, ...), condition=%wide.region_18.19_spmd, body=%wide.region_17.18_spmd.sunk | while | flops 6147 | bytes 49285 | solution.py:155
  120.6 9.4 %all_gather.27 = f32[4,3,3,8,128]{4,3,2,1,0:T(8,128)S(1)} all-gather(f32[1,3,3,8,128]{4,3,2,1,0:T(8,128)S(1)} %bitcast_divide_fusion), channel_id=1, replica_groups=mesh['gx'=2,'gy'=4,'gz'=4] {'gz'}, dimensions={0}, use_global_device_ids=true | all-gather | bytes 184320 | tf_op jit(solution)/shard_map/all_gather | solution.py:42
  130.4 6.7 %all_gather.28 = f32[4,8,128]{2,1,0:T(8,128)S(1)} all-gather(f32[1,8,128]{2,1,0:T(8,128)S(1)} %get-tuple-element.1172), channel_id=1, replica_groups=mesh['gx'=2,'gy'=4,'gz'=4] {'gz'}, dimensions={0}, use_global_device_ids=true | all-gather | bytes 20480 | tf_op jit(solution)/shard_map/all_gather | solution.py:42
  137.1 8.7 %all_gather.29 = f32[4,8,128]{2,1,0:T(8,128)S(1)} all-gather(f32[1,8,128]{2,1,0:T(8,128)S(1)} %get-tuple-element.1171), channel_id=1, replica_groups=mesh['gx'=2,'gy'=4,'gz'=4] {'gz'}, dimensions={0}, use_global_device_ids=true | all-gather | bytes 20480 | tf_op jit(solution)/shard_map/all_gather | solution.py:42
  146.0 2.0 %multiply_add_fusion = (f32[64,8,128]{2,1,0:T(8,128)}, f32[64,8,128]{2,1,0:T(8,128)}) fusion(pred[64,8,128]{2,1,0:T(8,128)(4,1)S(1)} %get-tuple-element.1090, pred[64,8,128]{2,1,0:T(8,128)(4,1)S(1)} %get-tuple-element.1089, pred[64,8,128]{2,1,0:T(8,128)(4,1)S(1)} %get-tuple-element.1088, pred[64,8,128]{2,1,0:T(8,128)(4,1)S(1)} %get-tuple-element.1087, ...), kind=kLoop, calls=%fused_computation.135 | loop fusion | flops 2490368 | bytes 1441792 | tf_op jit(solution)/shard_map/add | solution.py:89
  (549 shorter events, 25.4 us)
Async XLA Ops:
  0.6 20.2 %copy-start = (f32[64,8,128]{2,1,0:T(8,128)S(1)}, f32[64,8,128]{2,1,0:T(8,128)}, u32[]{:S(2)}) copy-start(f32[64,8,128]{2,1,0:T(8,128)} %param.22) | copy-start | bytes 786436
  5.1 15.7 %collective-permute-start = (f32[2,64,1,128]{3,2,1,0:T(1,128)S(1)}, f32[2,64,1,128]{3,2,1,0:T(1,128)S(1)}, u32[]{:S(2)}, u32[]{:S(2)}) collective-permute-start(f32[2,64,1,128]{3,2,1,0:T(1,128)S(1)} %get-tuple-element.1125), channel_id=1, source_target_pairs={{0,16},{1,17},{2,18},{3,19},{4,20},{5,21},{6,22},{7,23},{8,24},{9,... | collective-permute-start | bytes 196616 | tf_op jit(solution)/shard_map/ppermute | solution.py:34
  7.5 13.3 %collective-permute-start.1 = (f32[2,64,1,128]{3,2,1,0:T(1,128)S(1)}, f32[2,64,1,128]{3,2,1,0:T(1,128)S(1)}, u32[]{:S(2)}, u32[]{:S(2)}) collective-permute-start(f32[2,64,1,128]{3,2,1,0:T(1,128)S(1)} %get-tuple-element.1126), channel_id=1, source_target_pairs={{16,0},{17,1},{18,2},{19,3},{20,4},{21,5},{22,6},{23,7},{24,8},{25... | collective-permute-start | bytes 196616 | tf_op jit(solution)/shard_map/ppermute | solution.py:35
  21.7 6.0 %collective-permute-start.2 = (f32[2,64,10,1]{1,0,3,2:T(2,128)S(1)}, f32[2,64,10,1]{1,0,3,2:T(2,128)S(1)}, u32[]{:S(2)}, u32[]{:S(2)}) collective-permute-start(f32[2,64,10,1]{1,0,3,2:T(2,128)S(1)} %copy.14), channel_id=1, source_target_pairs={{0,4},{4,8},{8,12},{1,5},{5,9},{9,13},{2,6},{6,10},{10,14},{3,7},{... | collective-permute-start | bytes 15368 | tf_op jit(solution)/shard_map/ppermute | solution.py:34
  26.4 5.6 %collective-permute-start.3 = (f32[2,64,10,1]{1,0,3,2:T(2,128)S(1)}, f32[2,64,10,1]{1,0,3,2:T(2,128)S(1)}, u32[]{:S(2)}, u32[]{:S(2)}) collective-permute-start(f32[2,64,10,1]{1,0,3,2:T(2,128)S(1)} %copy.15), channel_id=1, source_target_pairs={{4,0},{8,4},{12,8},{5,1},{9,5},{13,9},{6,2},{10,6},{14,10},{7,3},{... | collective-permute-start | bytes 15368 | tf_op jit(solution)/shard_map/ppermute | solution.py:35
  32.6 5.0 %collective-permute-start.4 = (f32[2,1,10,130]{3,2,1,0:T(8,128)S(1)}, f32[2,1,10,130]{3,2,1,0:T(8,128)S(1)}, u32[]{:S(2)}, u32[]{:S(2)}) collective-permute-start(f32[2,1,10,130]{3,2,1,0:T(8,128)S(1)} %get-tuple-element.1105), channel_id=1, source_target_pairs={{0,1},{1,2},{2,3},{4,5},{5,6},{6,7},{8,9},{9,10},{10,11},{12,13},{... | collective-permute-start | bytes 31208 | tf_op jit(solution)/shard_map/ppermute | solution.py:34
  36.0 5.8 %collective-permute-start.5 = (f32[2,1,10,130]{3,2,1,0:T(8,128)S(1)}, f32[2,1,10,130]{3,2,1,0:T(8,128)S(1)}, u32[]{:S(2)}, u32[]{:S(2)}) collective-permute-start(f32[2,1,10,130]{3,2,1,0:T(8,128)S(1)} %get-tuple-element.1106), channel_id=1, source_target_pairs={{1,0},{2,1},{3,2},{5,4},{6,5},{7,6},{9,8},{10,9},{11,10},{13,12},{... | collective-permute-start | bytes 31208 | tf_op jit(solution)/shard_map/ppermute | solution.py:35
  37.5 27.5 %copy-start.2 = (f32[3,3]{1,0:T(4,128)}, f32[3,3]{1,0:T(4,128)S(1)}, u32[]{:S(2)}) copy-start(f32[3,3]{1,0:T(4,128)S(1)} %fusion.76) | copy-start | bytes 112
  55.4 25.6 %copy-start.1 = (f32[64,8,128]{2,1,0:T(8,128)S(1)}, f32[64,8,128]{2,1,0:T(8,128)}, u32[]{:S(2)}) copy-start(f32[64,8,128]{2,1,0:T(8,128)} %param.23) | copy-start | bytes 786436
  83.1 2.6 %collective-permute-start.6 = (f32[2,64,1,128]{3,2,1,0:T(1,128)S(1)}, f32[2,64,1,128]{3,2,1,0:T(1,128)S(1)}, u32[]{:S(2)}, u32[]{:S(2)}) collective-permute-start(f32[2,64,1,128]{3,2,1,0:T(1,128)S(1)} %get-tuple-element.1119), channel_id=1, source_target_pairs={{0,16},{1,17},{2,18},{3,19},{4,20},{5,21},{6,22},{7,23},{8,24},{9,... | collective-permute-start | bytes 196616 | tf_op jit(solution)/shard_map/ppermute | solution.py:34
  84.4 3.1 %collective-permute-start.7 = (f32[2,64,1,128]{3,2,1,0:T(1,128)S(1)}, f32[2,64,1,128]{3,2,1,0:T(1,128)S(1)}, u32[]{:S(2)}, u32[]{:S(2)}) collective-permute-start(f32[2,64,1,128]{3,2,1,0:T(1,128)S(1)} %get-tuple-element.1120), channel_id=1, source_target_pairs={{16,0},{17,1},{18,2},{19,3},{20,4},{21,5},{22,6},{23,7},{24,8},{25... | collective-permute-start | bytes 196616 | tf_op jit(solution)/shard_map/ppermute | solution.py:35
  88.5 5.3 %collective-permute-start.8 = (f32[2,64,10,1]{1,0,3,2:T(2,128)S(1)}, f32[2,64,10,1]{1,0,3,2:T(2,128)S(1)}, u32[]{:S(2)}, u32[]{:S(2)}) collective-permute-start(f32[2,64,10,1]{1,0,3,2:T(2,128)S(1)} %copy.18), channel_id=1, source_target_pairs={{0,4},{4,8},{8,12},{1,5},{5,9},{9,13},{2,6},{6,10},{10,14},{3,7},{... | collective-permute-start | bytes 15368 | tf_op jit(solution)/shard_map/ppermute | solution.py:34
  92.3 5.6 %collective-permute-start.9 = (f32[2,64,10,1]{1,0,3,2:T(2,128)S(1)}, f32[2,64,10,1]{1,0,3,2:T(2,128)S(1)}, u32[]{:S(2)}, u32[]{:S(2)}) collective-permute-start(f32[2,64,10,1]{1,0,3,2:T(2,128)S(1)} %copy.19), channel_id=1, source_target_pairs={{4,0},{8,4},{12,8},{5,1},{9,5},{13,9},{6,2},{10,6},{14,10},{7,3},{... | collective-permute-start | bytes 15368 | tf_op jit(solution)/shard_map/ppermute | solution.py:35
  98.5 3.5 %collective-permute-start.10 = (f32[2,1,10,130]{3,2,1,0:T(8,128)S(1)}, f32[2,1,10,130]{3,2,1,0:T(8,128)S(1)}, u32[]{:S(2)}, u32[]{:S(2)}) collective-permute-start(f32[2,1,10,130]{3,2,1,0:T(8,128)S(1)} %get-tuple-element.1103), channel_id=1, source_target_pairs={{0,1},{1,2},{2,3},{4,5},{5,6},{6,7},{8,9},{9,10},{10,11},{12,13},{... | collective-permute-start | bytes 31208 | tf_op jit(solution)/shard_map/ppermute | solution.py:34
  100.4 5.8 %collective-permute-start.11 = (f32[2,1,10,130]{3,2,1,0:T(8,128)S(1)}, f32[2,1,10,130]{3,2,1,0:T(8,128)S(1)}, u32[]{:S(2)}, u32[]{:S(2)}) collective-permute-start(f32[2,1,10,130]{3,2,1,0:T(8,128)S(1)} %get-tuple-element.1104), channel_id=1, source_target_pairs={{1,0},{2,1},{3,2},{5,4},{6,5},{7,6},{9,8},{10,9},{11,10},{13,12},{... | collective-permute-start | bytes 31208 | tf_op jit(solution)/shard_map/ppermute | solution.py:35
  114.3 15.7 %copy-start.3 = (f32[3,3]{1,0:T(4,128)S(1)}, f32[3,3]{1,0:T(4,128)}, u32[]{:S(2)}) copy-start(f32[3,3]{1,0:T(4,128)} %copy-done.2) | copy-start | bytes 112
where the time goes:
time: 148 us
  blocking collectives  49.6 us (34%)
  other arithmetic  41.5 us (28%)
  starting transfers between devices  24.9 us (17%)
  waiting for transfers between devices  17.9 us (12%)
  loops' own time  6.68 us (5%)
  local copies, waits for them, and re-layouts  5.58 us (4%)
  between operations  1.76 us (1%)
    all_gather x6, blocking collectives, carried_in(): pieces = jax.tree.map(lambda part: lax.all_gather(part, axis), value)  49.6 us
    ppermute x6, waiting for transfers between devices, padded(): after = lax.ppermute(initial, axis, down)  17.5 us
    ppermute x6, starting transfers between devices, padded(): before = lax.ppermute(last, axis, up)  16.8 us
    scatter-add x1, other arithmetic, per_device(): plane = jnp.zeros((row_count, col_count), jnp.float32).at[emitter_spot //...  11.2 us
    ppermute x6, starting transfers between devices, padded(): after = lax.ppermute(initial, axis, down)  8.13 us
    neg x4, other arithmetic, assemble(): return (-z_gain[:-1], diagonal, -z_gain[1:], -residual)  7.77 us
    mul x2, other arithmetic, flow_factor(): return sat_conduct * jnp.sqrt(effective) * inner_term * inner_term  5.4 us
    dynamic_update_slice x248, other arithmetic, block_reduce(): lax.scan(forward, (first_a[1], first_c[1], first_d[1]), (lower[2:], diago...  3.72 us
  transfers between devices with their start and end apart: 12, of which 6 were waited for; matrix products, arithmetic and copies ran while one was open for 9% of the time, Pallas kernels for 0%

commit v1 on v0

v1 whole, which is shorter than its diff:
```python
import functools

import jax
import jax.numpy as jnp
from jax import lax
from jax.experimental import pallas as pl
from jax.experimental.pallas import tpu as pltpu
from jax.sharding import PartitionSpec as P

DRIP = 30

ALPHA_TABLE = (3.6, 2.0, 1.9, 1.0, 5.9, 1.6)
SHAPE_TABLE = (1.56, 1.41, 1.31, 1.23, 1.48, 1.37)
RESIDUAL_TABLE = (0.078, 0.067, 0.095, 0.089, 0.1, 0.034)
SATURATED_TABLE = (0.43, 0.45, 0.41, 0.43, 0.39, 0.46)
CONDUCT_TABLE = (0.2496, 0.108, 0.0624, 0.0168, 0.3144, 0.06)
layer_height = 0.01
column_width = 2.0
time_step = 2.0
storage_floor = 0.001
emitter_flow = 0.096
vertical_gain = 1.0 / (layer_height * layer_height)
gravity_gain = 1.0 / layer_height
lateral_gain = 1.0 / (column_width * column_width)
storage_gain = 1.0 / time_step
emitter_rate = emitter_flow / (column_width * column_width * layer_height)

POWER_TABLE = tuple(n - 1.0 for n in SHAPE_TABLE)
M_TABLE = tuple(1.0 - 1.0 / n for n in SHAPE_TABLE)
SPREAD_TABLE = tuple(s - r for s, r in zip(SATURATED_TABLE, RESIDUAL_TABLE))
CAP_TABLE = tuple(
    storage_gain * s * a * p for s, a, p in zip(SPREAD_TABLE, ALPHA_TABLE, POWER_TABLE)
)
floor_gain = storage_floor * storage_gain
half_lateral = 0.5 * lateral_gain

ROWS, LANES = 8, 128
F32 = jnp.float32
SLOT = 40
PLANES = 9
SIDE = 2
PACK = -(-(PLANES * (ROWS + SIDE)) // ROWS) * ROWS
UNROLL = 4


def roll(value, shift, axis=1):
    size = value.shape[axis]
    shift = shift % size
    return value if shift == 0 else pltpu.roll(value, shift, axis)


def tile(z):
    return pl.ds(pl.multiple_of(z * ROWS, ROWS), ROWS)


def line(row, count):
    return pl.ds(row, count, stride=ROWS)


def iota(shape, dim):
    return lax.broadcasted_iota(jnp.int32, shape, dim)


def look_up(kinds, *tables):
    chosen = [kinds == float(number) for number in range(1, len(ALPHA_TABLE))]
    found = []
    for table in tables:
        value = jnp.full(kinds.shape, table[0], F32)
        for number, mask in enumerate(chosen, 1):
            value = jnp.where(mask, table[number], value)
        found.append(value)
    return found


def retention(head, alpha, power, m_shape, conduct):
    wet = head >= 0.0
    scaled = alpha * jnp.abs(head)
    raised = jnp.where(wet, 0.0, jnp.exp(power * jnp.log(scaled)))
    lifted = 1.0 + raised * scaled
    root = jnp.exp((-0.5 * m_shape) * jnp.log(lifted))
    effective = root * root
    product = raised * effective
    inner = 1.0 - product
    return conduct * root * inner * inner, effective, product / lifted


def saturation(head, alpha, power, m_shape):
    wet = head >= 0.0
    scaled = alpha * jnp.abs(head)
    raised = jnp.where(wet, 0.0, jnp.exp(power * jnp.log(scaled)))
    return jnp.exp(-m_shape * jnp.log(1.0 + raised * scaled))


def raw_retention(head, scale, kinds):
    alpha, power, m_shape, conduct, cap = look_up(
        kinds, ALPHA_TABLE, POWER_TABLE, M_TABLE, CONDUCT_TABLE, CAP_TABLE
    )
    k_value, unused, shape = retention(head, alpha, power, m_shape, conduct * scale)
    return k_value, cap * shape + floor_gain


def each_layer(count, body, carry):
    step = UNROLL if count % UNROLL == 0 else 1

    def several(chunk, carry):
        for inner in range(step):
            carry = body(chunk * step + inner, carry)
        return carry

    return lax.fori_loop(0, count // step, several, carry)


def vertical(z, count, k_ref, h_ref, above):
    below = jnp.minimum(z + 1, count - 1)
    inside = jnp.where(z < count - 1, 0.5, 0.0)
    face = inside * (k_ref[tile(z), :] + k_ref[tile(below), :])
    flux = face * ((h_ref[tile(z), :] - h_ref[tile(below), :]) * vertical_gain + gravity_gain)
    return face * vertical_gain, above - flux, flux


def inner_lateral(k_here, h_here):
    gain = jnp.zeros_like(k_here)
    inflow = jnp.zeros_like(k_here)
    for axis, size in ((0, ROWS), (1, LANES)):
        inside = jnp.where(iota(k_here.shape, axis) < size - 1, half_lateral, 0.0)
        face = inside * (k_here + roll(k_here, -1, axis))
        flux = face * (h_here - roll(h_here, -1, axis))
        gain = gain + face + roll(face, 1, axis)
        inflow = inflow - flux + roll(flux, 1, axis)
    return gain, inflow


def edge_weights(gx, gy, y_count):
    row, lane = iota((ROWS, LANES), 0), iota((ROWS, LANES), 1)
    x_side = row == jnp.where(gx == 0, ROWS - 1, 0)
    west = jnp.where(gy > 0, 0, -1)
    east = jnp.where(gy < y_count - 1, LANES - 1, -1)
    y_side = (lane == west) | (lane == east)
    return jnp.where(x_side, half_lateral, 0.0), jnp.where(y_side, half_lateral, 0.0)


def edge_terms(z, k_here, h_here, weights, side_refs):
    x_k, x_h, y_k, y_h = side_refs
    x_weight, y_weight = weights
    x_face = x_weight * (k_here + x_k[pl.ds(z, 1), :])
    y_face = y_weight * (k_here + y_k[tile(z), :])
    inflow = x_face * (x_h[pl.ds(z, 1), :] - h_here) + y_face * (y_h[tile(z), :] - h_here)
    return x_face + y_face, inflow


def spread_columns(packed, out_ref, count):
    j = iota(packed.shape, 1) & 3
    swapped = jnp.where(j == 2, roll(packed, 1), roll(packed, -1))
    for x in range(ROWS):
        out_ref[line(x, count), :] = roll(swapped, -(4 * (x + 1) + 2))


def eliminations(count):
    order, nodes = [], list(range(count))
    while len(nodes) > 2:
        gone = set()
        for place in range(1, len(nodes) - 1, 2):
            order.append((nodes[place], nodes[place - 1], nodes[place + 1], place == 1))
            gone.add(nodes[place])
        nodes = [node for node in nodes if node not in gone]
    return order


def at(node):
    return slice(node * ROWS, (node + 1) * ROWS)


def reduce_block(count, streams):
    order = eliminations(count)
    carried = [None] * len(streams)
    for place, (j, i, k, opening) in enumerate(order):
        closing = place + 1 == len(order) or order[place + 1][3]
        for s, (e, r, g, t_up, t_down, w) in enumerate(streams):
            e_j, r_j, g_up, g_down = e[at(j), :], r[at(j), :], g[at(i), :], g[at(j), :]
            inverse = 1.0 / (e_j + (g_up + g_down))
            up, down = g_up * inverse, g_down * inverse
            t_up[at(j), :] = up
            t_down[at(j), :] = down
            w[at(j), :] = r_j * inverse
            e_i, r_i = e[at(i), :] + up * e_j, r[at(i), :] + up * r_j
            if not opening:
                e_i, r_i = e_i + carried[s][0], r_i + carried[s][1]
            e[at(i), :] = e_i
            r[at(i), :] = r_i
            g[at(i), :] = g_up * down
            carried[s] = (down * e_j, down * r_j)
            if closing:
                e[at(k), :] = e[at(k), :] + carried[s][0]
                r[at(k), :] = r[at(k), :] + carried[s][1]


def substitute_block(count, streams):
    for j, i, k, unused in reversed(eliminations(count)):
        for x, t_up, t_down, w in streams:
            x[at(j), :] = w[at(j), :] + t_up[at(j), :] * x[at(i), :] + t_down[at(j), :] * x[at(k), :]


def write_port(count, out_ref, e, r, g, k, h, rows, start, is_bottom):
    first, last = slice(0, rows), slice((count - 1) * ROWS, (count - 1) * ROWS + rows)
    open_face = jnp.where(is_bottom, 1.0, 0.0) * k[last, :]
    port = (
        e[first, :],
        e[last, :] + open_face * vertical_gain,
        g[first, :],
        r[first, :],
        r[last, :] - open_face * (h[last, :] * vertical_gain + gravity_gain),
        k[first, :],
        k[last, :],
        h[first, :],
        h[last, :],
    )
    for place, value in enumerate(port):
        out_ref[start + place * rows : start + (place + 1) * rows, :] = value


def solve_chain(blocks, gathered, rows, start):
    def port(block, place):
        low = block * PACK + start + place * rows
        return gathered[low : low + rows, :]

    e, r, links = [], [], []
    for block in range(blocks):
        e += [port(block, 0), port(block, 1)]
        r += [port(block, 3), port(block, 4)]
        links.append(port(block, 2))
        if block < blocks - 1:
            face = 0.5 * (port(block, 6) + port(block + 1, 5))
            flux = face * ((port(block, 8) - port(block + 1, 7)) * vertical_gain + gravity_gain)
            links.append(face * vertical_gain)
            r[-1] = r[-1] - flux
            links_flux = flux
        if block > 0:
            r[-2] = r[-2] + previous
        previous = links_flux if block < blocks - 1 else None
    count = 2 * blocks
    middle = count // 2
    steps = {}

    def fold(node, target, link):
        inverse = 1.0 / (e[node] + link)
        share = link * inverse
        e[target] = e[target] + share * e[node]
        r[target] = r[target] + share * r[node]
        steps[node] = (target, share, r[node] * inverse)

    for step in range(middle):
        fold(step, step + 1, links[step])
        if count - 1 - step > middle:
            fold(count - 1 - step, count - 2 - step, links[count - 2 - step])
    found = {middle: r[middle] / e[middle]}
    for step in range(middle):
        for node in (middle - 1 - step, middle + 1 + step):
            if node in steps:
                target, share, rest = steps[node]
                found[node] = rest + share * found[target]
    return [found[node] for node in range(count)]


def gather_ports(gz, blocks, own, received, gathered):
    for offset, part in enumerate((own, *received)):
        gathered[pl.ds(pl.multiple_of((gz ^ offset) * PACK, ROWS), PACK), :] = part[...]


def own_ends(gz, blocks, found, rows, ends_ref):
    for block in range(blocks):
        ends_ref[block * 2 * ROWS : block * 2 * ROWS + rows, :] = found[2 * block]
        ends_ref[(block * 2 + 1) * ROWS : (block * 2 + 1) * ROWS + rows, :] = found[2 * block + 1]
    return ends_ref[tile(gz * 2), :], ends_ref[tile(gz * 2 + 1), :]


def pack_kernel(h, ks, kinds, cells, columns, rows_out, counts, kind_f):
    gx = lax.axis_index("gx")
    size = h.shape[0]
    count = size // ROWS
    spots = cells[...]
    emitters = spots.shape[1]
    in_row = jnp.where(iota((ROWS, emitters), 0) == (spots >> 7), 1.0, 0.0)
    in_lane = jnp.where(iota((LANES, emitters), 0) == (spots & (LANES - 1)), 1.0, 0.0)
    plane = lax.dot_general(
        in_row.astype(jnp.bfloat16),
        in_lane.astype(jnp.bfloat16),
        (((1,), (1,)), ((), ())),
        preferred_element_type=F32,
    )
    counts[...] = plane
    kind_f[...] = kinds[...].astype(F32)
    group = iota((count, LANES), 1) >> 2
    packed = jnp.zeros((count, LANES), F32)
    for place, source in enumerate((h, ks, kind_f)):
        for x in range(ROWS):
            slot = x + 1 + place * (SLOT // 4)
            moved = roll(source[line(x, count), :], 4 * slot + 2)
            packed = jnp.where(group == slot, moved, packed)
    columns[0:count, :] = packed
    group8 = iota((1, LANES), 1) >> 2
    spot_row = jnp.zeros((1, LANES), F32)
    for x in range(ROWS):
        spot_row = jnp.where(group8 == x + 1, roll(counts[x : x + 1, :], 4 * (x + 1) + 2), spot_row)
    columns[count : count + ROWS, :] = jnp.broadcast_to(spot_row, (ROWS, LANES))
    low = gx == 0
    for place, source in enumerate((h, ks, kind_f)):
        for depth in range(2):
            picked = jnp.where(
                low, source[line(ROWS - 1 - depth, count), :], source[line(depth, count), :]
            )
            start = (2 * place + depth) * count
            rows_out[start : start + count, :] = picked
    edge = jnp.where(low, counts[ROWS - 1 : ROWS, :], counts[0:1, :])
    rows_out[6 * count : 6 * count + ROWS, :] = jnp.broadcast_to(edge, (ROWS, LANES))


def local_kernel(h, ks, kinds, counts, k_out, e_out, r_out, g_out, se_out, alpha_out, power_out, m_out, spread_out, conduct_out):
    count = h.shape[0] // ROWS
    is_top = lax.axis_index("gz") == 0

    def first(z, unused):
        head = h[tile(z), :]
        alpha, power, m_shape, spread, conduct, cap = look_up(
            kinds[tile(z), :].astype(F32), ALPHA_TABLE, POWER_TABLE, M_TABLE, SPREAD_TABLE, CONDUCT_TABLE, CAP_TABLE
        )
        conduct = conduct * ks[tile(z), :]
        k_value, effective, shape = retention(head, alpha, power, m_shape, conduct)
        k_out[tile(z), :] = k_value
        e_out[tile(z), :] = cap * shape + floor_gain
        se_out[tile(z), :] = effective
        alpha_out[tile(z), :] = alpha
        power_out[tile(z), :] = power
        m_out[tile(z), :] = m_shape
        spread_out[tile(z), :] = spread
        conduct_out[tile(z), :] = conduct
        return unused

    each_layer(count, first, 0)
    source = jnp.where(is_top, emitter_rate, 0.0) * counts[...]

    def second(z, above):
        link, inflow, flux = vertical(z, count, k_out, h, above)
        gain, sideways = inner_lateral(k_out[tile(z), :], h[tile(z), :])
        g_out[tile(z), :] = link
        e_out[tile(z), :] = e_out[tile(z), :] + gain
        r_out[tile(z), :] = inflow + sideways
        return flux

    each_layer(count, second, jnp.zeros((ROWS, LANES), F32))
    r_out[at(DRIP), :] = r_out[at(DRIP), :] + source


def merge_halo(gx, gy, from_even, from_odd, far_even, far_odd):
    lane = iota(from_even.shape, 1)
    even = (gy & 1) == 0
    j = lane & 3

    def both(e_part, o_part):
        left = jnp.where(even, o_part[...], e_part[...])
        right = jnp.where(even, e_part[...], o_part[...])
        return jnp.where(j < 2, left, right)

    near, far = both(from_even, from_odd), both(far_even, far_odd)
    low = gx == 0
    corner = jnp.where(low, 9, 0)
    group = lane >> 2
    hit = (group == corner) | (group == corner + SLOT // 4) | (group == corner + SLOT // 2)
    return jnp.where(hit, jnp.where(low, roll(far, 32), roll(far, -32)), near)


def unpack(packed):
    used = iota(packed.shape, 1) < SLOT
    return [jnp.where(used, roll(packed, -SLOT * place), 0.0) for place in range(3)]


def side_lateral(gx, gy, y_count, near_k, near_h, row1, row2, col, own):
    lane = iota(near_k.shape, 1)
    low = gx == 0

    def pair(here, there, weight):
        face = weight * (here[0] + there[0])
        return face, face * (there[1] - here[1])

    def moved(cells, shift):
        return [roll(part, shift) for part in cells]

    def pick(mask, yes, no):
        return [jnp.where(mask, a, b) for a, b in zip(yes, no)]

    corner_west = pick(low, moved(col, -37), moved(col, -1))
    corner_east = pick(low, moved(col, LANES - 1 - 38), moved(col, LANES - 1 - 2))
    west = pick(lane == 0, corner_west, moved(row1, 1))
    east = pick(lane == LANES - 1, corner_east, moved(row1, -1))
    west_weight = jnp.where((lane > 0) | (gy > 0), half_lateral, 0.0)
    east_weight = jnp.where((lane < LANES - 1) | (gy < y_count - 1), half_lateral, 0.0)
    row_terms = [
        pair(row1, (near_k, near_h), half_lateral),
        pair(row1, row2, half_lateral),
        pair(row1, west, west_weight),
        pair(row1, east, east_weight),
    ]
    j = lane & 3
    p = lane >> 2
    less_weight = jnp.where((p > 1) | (gx == 1), half_lateral, 0.0)
    more_weight = jnp.where((p < 8) | (gx == 0), half_lateral, 0.0)
    inner = pick(j == 1, moved(own, -1), moved(own, 1))
    outer = pick(j == 1, moved(col, 1), moved(col, -1))
    col_terms = [
        pair(col, inner, half_lateral),
        pair(col, outer, half_lateral),
        pair(col, moved(col, 4), less_weight),
        pair(col, moved(col, -4), more_weight),
    ]
    total = []
    for terms in (row_terms, col_terms):
        total.append((sum(t[0] for t in terms), sum(t[1] for t in terms)))
    return total


def first_kernel(
    y_count, z_count, h, k, e_in, r_in, g_in, rows, columns, from_even, from_odd, far_even, far_odd,
    port, t_up, t_down, w, s_up, s_down, s_w, col_raw,
    e, r, g, se, sr, sg, sk, sh, y_k, y_h, x_k, x_h,
):
    gx, gy, gz = lax.axis_index("gx"), lax.axis_index("gy"), lax.axis_index("gz")
    size = h.shape[0]
    count = size // ROWS
    is_top, is_bottom = gz == 0, gz == z_count - 1

    halo = merge_halo(gx, gy, from_even, from_odd, far_even, far_odd)
    col_raw[...] = halo
    col_h, col_s, col_c = unpack(col_raw[0:count, :])
    own_h, own_s, own_c = unpack(columns[0:count, :])

    def raw_row(place):
        return rows[place * count : (place + 1) * count, :]

    row_k, row_e = raw_retention(raw_row(0), raw_row(2), raw_row(4))
    far_k, unused = raw_retention(raw_row(1), raw_row(3), raw_row(5))
    col_k, col_e = raw_retention(col_h, col_s, col_c)
    own_k, unused2 = raw_retention(own_h, own_s, own_c)
    x_k[...] = row_k
    x_h[...] = raw_row(0)
    spread_columns(col_k, y_k, count)
    spread_columns(col_h, y_h, count)
    low = gx == 0
    near_k = jnp.where(low, k[line(ROWS - 1, count), :], k[line(0, count), :])
    near_h = jnp.where(low, h[line(ROWS - 1, count), :], h[line(0, count), :])
    (row_gain, row_in), (col_gain, col_in) = side_lateral(
        gx, gy, y_count, near_k, near_h, (row_k, raw_row(0)), (far_k, raw_row(1)), (col_k, col_h), (own_k, own_h)
    )
    source_at = jnp.where(is_top & (iota((count, LANES), 0) == DRIP), emitter_rate, 0.0)
    row_in = row_in + source_at * rows[6 * count : 6 * count + 1, :]
    col_in = col_in + source_at * col_raw[count : count + 1, :]
    se[...] = jnp.ones_like(se)
    sr[...] = jnp.zeros_like(sr)
    sk[...] = jnp.zeros_like(sk)
    sh[...] = jnp.zeros_like(sh)
    for place, (gain, inflow, k_part, h_part) in enumerate(
        ((row_gain + row_e, row_in, row_k, raw_row(0)), (col_gain + col_e, col_in, col_k, col_h))
    ):
        se[line(place, count), :] = gain
        sr[line(place, count), :] = inflow
        sk[line(place, count), :] = k_part
        sh[line(place, count), :] = h_part

    weights = edge_weights(gx, gy, y_count)

    def layer(z, above):
        gain, inflow = edge_terms(z, k[tile(z), :], h[tile(z), :], weights, (x_k, x_h, y_k, y_h))
        e[tile(z), :] = e_in[tile(z), :] + gain
        r[tile(z), :] = r_in[tile(z), :] + inflow
        g[tile(z), :] = g_in[tile(z), :]
        link, side_in, flux = vertical(z, count, sk, sh, above)
        sg[tile(z), :] = link
        sr[tile(z), :] = sr[tile(z), :] + side_in
        return flux

    each_layer(count, layer, jnp.zeros((ROWS, LANES), F32))
    reduce_block(count, ((e, r, g, t_up, t_down, w), (se, sr, sg, s_up, s_down, s_w)))
    write_port(count, port, e, r, g, k, h, ROWS, 0, is_bottom)
    write_port(count, port, se, sr, sg, sk, sh, SIDE, PLANES * ROWS, is_bottom)
    used = PLANES * (ROWS + SIDE)
    if used < PACK:
        port[used:PACK, :] = jnp.zeros((PACK - used, LANES), F32)


def second_kernel(y_count, z_count, *refs):
    own, received, refs = refs[0], refs[1:z_count], refs[z_count:]
    (
        t_up0, t_down0, w0, s_up, s_down, s_w, rows, col_raw, counts, h_in, conduct, alpha, power, m_shape, spread, se_old,
        port, t_up, t_down, w, h,
        gathered, ends, x, side_x, k, e, r, g, y_k, y_h, x_k, x_h,
    ) = refs
    gx, gy, gz = lax.axis_index("gx"), lax.axis_index("gy"), lax.axis_index("gz")
    count = h.shape[0] // ROWS
    is_top, is_bottom = gz == 0, gz == z_count - 1
    gather_ports(gz, z_count, own, received, gathered)
    side_x[at(0), :] = jnp.zeros((ROWS, LANES), F32)
    side_x[at(count - 1), :] = jnp.zeros((ROWS, LANES), F32)
    found = solve_chain(z_count, gathered, ROWS, 0)
    x[at(0), :], x[at(count - 1), :] = own_ends(gz, z_count, found, ROWS, ends)
    found = solve_chain(z_count, gathered, SIDE, PLANES * ROWS)
    side_first, side_last = own_ends(gz, z_count, found, SIDE, ends)
    side_x[0:SIDE, :] = side_first[0:SIDE, :]
    side_x[(count - 1) * ROWS : (count - 1) * ROWS + SIDE, :] = side_last[0:SIDE, :]
    substitute_block(count, ((x, t_up0, t_down0, w0), (side_x, s_up, s_down, s_w)))

    def raw_row(place):
        return rows[place * count : (place + 1) * count, :]

    row_h = raw_row(0) + side_x[line(0, count), :]
    col_h, col_s, col_c = unpack(col_raw[0:count, :])
    col_h = col_h + side_x[line(1, count), :]
    x_k[...] = raw_retention(row_h, raw_row(2), raw_row(4))[0]
    x_h[...] = row_h
    spread_columns(raw_retention(col_h, col_s, col_c)[0], y_k, count)
    spread_columns(col_h, y_h, count)

    def first(z, unused):
        here = tile(z)
        head = h_in[here, :] + x[here, :]
        h[here, :] = head
        k_value, effective, shape = retention(head, alpha[here, :], power[here, :], m_shape[here, :], conduct[here, :])
        k[here, :] = k_value
        spread_here = spread[here, :]
        cap = (storage_gain * spread_here) * (alpha[here, :] * power[here, :])
        e[here, :] = cap * shape + floor_gain
        r[here, :] = (-storage_gain * spread_here) * (effective - se_old[here, :])
        return unused

    each_layer(count, first, 0)
    weights = edge_weights(gx, gy, y_count)

    def second(z, above):
        here = tile(z)
        link, inflow, flux = vertical(z, count, k, h, above)
        gain, sideways = inner_lateral(k[here, :], h[here, :])
        edge_gain, edge_in = edge_terms(z, k[here, :], h[here, :], weights, (x_k, x_h, y_k, y_h))
        g[here, :] = link
        e[here, :] = e[here, :] + (gain + edge_gain)
        r[here, :] = r[here, :] + (inflow + sideways + edge_in)
        return flux

    each_layer(count, second, jnp.zeros((ROWS, LANES), F32))
    source = jnp.where(is_top, emitter_rate, 0.0)
    r[at(DRIP), :] = r[at(DRIP), :] + source * counts[...]
    reduce_block(count, ((e, r, g, t_up, t_down, w),))
    write_port(count, port, e, r, g, k, h, ROWS, 0, is_bottom)
    used = PLANES * ROWS
    if used < PACK:
        port[used:PACK, :] = jnp.zeros((PACK - used, LANES), F32)


def last_kernel(z_count, *refs):
    own, received, refs = refs[0], refs[1:z_count], refs[z_count:]
    t_up, t_down, w, h_in, kinds, head, water, gathered, ends, x = refs
    gz = lax.axis_index("gz")
    count = h_in.shape[0] // ROWS
    gather_ports(gz, z_count, own, received, gathered)
    found = solve_chain(z_count, gathered, ROWS, 0)
    x[at(0), :], x[at(count - 1), :] = own_ends(gz, z_count, found, ROWS, ends)
    substitute_block(count, ((x, t_up, t_down, w),))

    def layer(z, unused):
        here = tile(z)
        pressure = h_in[here, :] + x[here, :]
        alpha, power, m_shape, spread, residual = look_up(
            kinds[here, :].astype(F32), ALPHA_TABLE, POWER_TABLE, M_TABLE, SPREAD_TABLE, RESIDUAL_TABLE
        )
        head[here, :] = pressure
        water[here, :] = residual + spread * saturation(pressure, alpha, power, m_shape)
        return unused

    each_layer(count, layer, 0)


def per_device(sizes, head_old, ks_scale, soil_class, emitter_cells):
    x_count, y_count, z_count = sizes
    count, rows, lanes = head_old.shape
    assert (rows, lanes, x_count) == (ROWS, LANES, 2) and count > DRIP
    assert z_count & (z_count - 1) == 0
    size = count * ROWS

    def array(length):
        return jax.ShapeDtypeStruct((length, LANES), F32)

    def buffer(length):
        return pltpu.VMEM((length, LANES), F32)

    def call(kernel, name, outs, scratch, flops, *operands):
        return pl.pallas_call(
            kernel,
            name=name,
            out_shape=[array(length) for length in outs],
            in_specs=[pl.BlockSpec(memory_space=pltpu.VMEM)] * len(operands),
            out_specs=[pl.BlockSpec(memory_space=pltpu.VMEM)] * len(outs),
            scratch_shapes=[buffer(length) for length in scratch],
            compiler_params=pltpu.CompilerParams(vmem_limit_bytes=24 << 20),
            cost_estimate=pl.CostEstimate(flops=flops, bytes_accessed=flops, transcendentals=0),
        )(*operands)

    h, ks, kinds = (value.reshape(size, LANES) for value in (head_old, ks_scale, soil_class))
    cells = emitter_cells.reshape(1, -1)
    columns, rows_out, counts = call(
        pack_kernel, "pack", (count + ROWS, 6 * count + ROWS, ROWS), (size,), 1 << 20, h, ks, kinds, cells
    )
    even = [(y ^ 1, y) for y in range(y_count) if y ^ 1 < y_count]
    odd = [(y, y + 1) for y in range(1, y_count - 1, 2)]
    odd += [(b, a) for a, b in odd]
    swap = [(0, 1), (1, 0)]
    from_even = lax.ppermute(columns, "gy", even)
    from_odd = lax.ppermute(columns, "gy", odd)
    side_rows = lax.ppermute(rows_out, "gx", swap)
    far_even = lax.ppermute(from_even, "gx", swap)
    far_odd = lax.ppermute(from_odd, "gx", swap)
    k, e, r, g, se_old, alpha, power, m_shape, spread, conduct = call(
        local_kernel, "local", (size,) * 10, (), 4 << 20, h, ks, kinds, counts
    )
    port, t_up, t_down, w, s_up, s_down, s_w, col_raw = call(
        functools.partial(first_kernel, y_count, z_count),
        "first",
        (PACK, *(size,) * 6, count + ROWS),
        (*(size,) * 9, size, count, count),
        4 << 20,
        h, k, e, r, g, side_rows, columns, from_even, from_odd, far_even, far_odd,
    )

    def exchange(value):
        return [
            lax.ppermute(value, "gz", [(z, z ^ offset) for z in range(z_count)])
            for offset in range(1, z_count)
        ]

    port2, t_up, t_down, w, h1 = call(
        functools.partial(second_kernel, y_count, z_count),
        "second",
        (PACK, *(size,) * 4),
        (z_count * PACK, z_count * 2 * ROWS, *(size,) * 8, count, count),
        4 << 20,
        port, *exchange(port), t_up, t_down, w, s_up, s_down, s_w, side_rows, col_raw, counts, h, conduct, alpha, power, m_shape, spread, se_old,
    )
    head, water = call(
        functools.partial(last_kernel, z_count),
        "last",
        (size, size),
        (z_count * PACK, z_count * 2 * ROWS, size),
        4 << 20,
        port2, *exchange(port2), t_up, t_down, w, h1, kinds,
    )
    return head.reshape(head_old.shape), water.reshape(head_old.shape)


def solution(mesh):
    in_specs = (P("gz", "gx", "gy"), P("gz", "gx", "gy"), P("gz", "gx", "gy"), P("gx", "gy", None))
    out_specs = (P("gz", "gx", "gy"), P("gz", "gx", "gy"))
    sizes = tuple(mesh.shape[axis] for axis in ("gx", "gy", "gz"))
    return jax.shard_map(
        functools.partial(per_device, sizes),
        mesh=mesh, in_specs=in_specs, out_specs=out_specs, check_vma=False,
    )
```

time: 148 us -> 37.3 us (0.25)
  blocking collectives: 49.6 us -> 0 us
  other arithmetic: 41.5 us -> 0 us
  starting transfers between devices: 24.9 us -> 13.8 us
  Pallas kernels: 0 us -> 10.9 us
  waiting for transfers between devices: 17.9 us -> 8.17 us
  loops' own time: 6.68 us -> 0 us
  local copies, waits for them, and re-layouts: 5.58 us -> 3.52 us
    all_gather x6 -> x0, blocking collectives: 49.6 us -> none  [carried_in(): pieces = jax.tree.map(lambda part: lax.all_gather(part, axis), value)]
    scatter-add x1 -> x0, other arithmetic: 11.2 us -> none  [per_device(): plane = jnp.zeros((row_count, col_count), jnp.float32).at[emitter_spot //...]
    ppermute x12 -> x11, starting transfers between devices: 24.9 us -> 13.8 us  [the longest x6 7.11 us: exchange(): lax.ppermute(value, 'gz', [(z, z ^ offset) for z in range(z_count)])]
    pallas_call x0 -> x5, Pallas kernels: none -> 10.9 us  [call(): pl.pallas_call(kernel, name=name, out_shape=[array(length) for length in...]
    ppermute x12 -> x11, waiting for transfers between devices: 17.9 us -> 8.17 us  [the longest x6 6.22 us: exchange(): lax.ppermute(value, 'gz', [(z, z ^ offset) for z in range(z_count)])]
    mul x18 -> x0, other arithmetic: 8.82 us -> none  [the longest x2 5.4 us: flow_factor(): return sat_conduct * jnp.sqrt(effective) * inner_term * inner_term]
    neg x4 -> x0, other arithmetic: 7.77 us -> none  [assemble(): return (-z_gain[:-1], diagonal, -z_gain[1:], -residual)]
    another operation x8 -> x0, loops' own time: 6.68 us -> none  [the longest x2 3.59 us: block_reduce(): lax.scan(forward, (first_a[1], first_c[1], first_d[1]), (lower[2:], diago...]
  transfers between devices with their start and end apart: 12 -> 11, of which waited for: 6 -> 7; matrix products, arithmetic and copies ran while one was open for 9% -> 0% of each run, Pallas kernels for 0% -> 9%
where the time goes in v1:
time: 37.3 us; the launch traced here: 37.1 us
  starting transfers between devices  13.8 us (37%)
  Pallas kernels  10.9 us (29%)
  waiting for transfers between devices  8.17 us (22%)
  local copies, waits for them, and re-layouts  3.52 us (9%)
  between operations  0.71 us (2%)
    pallas_call x5, Pallas kernels, call(): pl.pallas_call(kernel, name=name, out_shape=[array(length) for length in...  10.9 us
    ppermute x6, starting transfers between devices, exchange(): lax.ppermute(value, 'gz', [(z, z ^ offset) for z in range(z_count)])  7.11 us
    ppermute x6, waiting for transfers between devices, exchange(): lax.ppermute(value, 'gz', [(z, z ^ offset) for z in range(z_count)])  6.22 us
    ppermute x1, starting transfers between devices, per_device(): from_even = lax.ppermute(columns, 'gy', even)  5.47 us
    unnamed x10, local copies, waits for them, and re-layouts  3.52 us
    ppermute x1, waiting for transfers between devices, per_device(): from_even = lax.ppermute(columns, 'gy', even)  1.93 us
  transfers between devices with their start and end apart: 11, of which 7 were waited for; matrix products, arithmetic and copies ran while one was open for 0% of the time, Pallas kernels for 9%

profile of v1, /device:TPU:0, one launch (start us, length us, event | category | flops | bytes accessed | tf_op | source)
XLA Modules:
  0.0 37.1 jit_solution(15915512136751941157)
XLA Ops:
  0.6 0.7 %copy-done.4 = s32[1,1,256]{2,1,0:T(1,128)S(1)} copy-done((s32[1,1,256]{2,1,0:T(1,128)S(1)}, s32[1,1,256]{2,1,0:T(1,128)}, u32[]{:S(2)}) %copy-start.4) | copy-done | bytes 1048
  1.3 0.9 %copy-done = f32[64,8,128]{2,1,0:T(8,128)S(1)} copy-done((f32[64,8,128]{2,1,0:T(8,128)S(1)}, f32[64,8,128]{2,1,0:T(8,128)}, u32[]{:S(2)}) %copy-start) | copy-done | bytes 262168
  2.3 0.9 %copy-done.1 = s32[64,8,128]{2,1,0:T(8,128)S(1)} copy-done((s32[64,8,128]{2,1,0:T(8,128)S(1)}, s32[64,8,128]{2,1,0:T(8,128)}, u32[]{:S(2)}) %copy-start.1) | copy-done | bytes 262168
  3.2 0.9 %copy-done.3 = f32[64,8,128]{2,1,0:T(8,128)S(1)} copy-done((f32[64,8,128]{2,1,0:T(8,128)S(1)}, f32[64,8,128]{2,1,0:T(8,128)}, u32[]{:S(2)}) %copy-start.3) | copy-done | bytes 262168
  4.2 0.3 pack.1
  4.5 0.6 %collective-permute-start = (f32[392,128]{1,0:T(8,128)S(1)}, f32[392,128]{1,0:T(8,128)S(1)}, u32[]{:S(2)}, u32[]{:S(2)}) collective-permute-start(f32[392,128]{1,0:T(8,128)S(1)} %get-tuple-element.35), channel_id=1, source_target_pairs={{0,16},{16,0},{1,17},{17,1},{2,18},{18,2},{3,19},{19,3},{4,20},{20... | collective-permute-start | bytes 602120 | tf_op jit(solution)/shard_map/ppermute | solution.py:614
  5.0 0.7 %collective-permute-start.2 = (f32[72,128]{1,0:T(8,128)S(1)}, f32[72,128]{1,0:T(8,128)S(1)}, u32[]{:S(2)}, u32[]{:S(2)}) collective-permute-start(f32[72,128]{1,0:T(8,128)S(1)} %get-tuple-element.36.columns), channel_id=1, source_target_pairs={{4,8},{8,4},{5,9},{9,5},{6,10},{10,6},{7,11},{11,7},{20,24},{24,20... | collective-permute-start | bytes 110600 | tf_op jit(solution)/shard_map/ppermute | solution.py:613
  5.7 5.5 %collective-permute-start.1 = (f32[72,128]{1,0:T(8,128)S(1)}, f32[72,128]{1,0:T(8,128)S(1)}, u32[]{:S(2)}, u32[]{:S(2)}) collective-permute-start(f32[72,128]{1,0:T(8,128)S(1)} %get-tuple-element.36.columns), channel_id=1, source_target_pairs={{4,0},{0,4},{12,8},{8,12},{5,1},{1,5},{13,9},{9,13},{6,2},{2,6},{1... | collective-permute-start | bytes 110600 | tf_op jit(solution)/shard_map/ppermute | solution.py:612
  11.2 0.0 collective-permute-done.2.from_odd
  11.2 0.0 collective-permute-start.4
  11.2 1.9 %collective-permute-done.1.from_even = f32[72,128]{1,0:T(8,128)S(1)} collective-permute-done((f32[72,128]{1,0:T(8,128)S(1)}, f32[72,128]{1,0:T(8,128)S(1)}, u32[]{:S(2)}, u32[]{:S(2)}) %collective-permute-start.1) | collective-permute-done | bytes 36896 | tf_op jit(solution)/shard_map/ppermute | solution.py:612
  13.1 0.0 collective-permute-start.3
  13.1 3.5 %local.1 = (f32[512,128]{1,0:T(8,128)S(1)}, f32[512,128]{1,0:T(8,128)S(1)}, f32[512,128]{1,0:T(8,128)S(1)}, f32[512,128]{1,0:T(8,128)S(1)}, f32[512,128]{1,0:T(8...) custom-call(f32[512,128]{1,0:T(8,128)S(1)} %bitcast.7, ...), custom_call_target="tpu_custom_call" | custom-call | flops 4194304 | bytes 4194304 | tf_op jit(solution)/shard_map/local/pallas_call | solution.py:592
  16.6 0.0 collective-permute-done.4.far_odd
  16.6 0.0 collective-permute-done.3.far_even
  16.6 0.0 collective-permute-done.rows.refs_10_
  16.6 1.5 %first.1 = (f32[96,128]{1,0:T(8,128)S(1)}, f32[512,128]{1,0:T(8,128)S(1)}, f32[512,128]{1,0:T(8,128)S(1)}, f32[512,128]{1,0:T(8,128)S(1)}, f32[512,128]{1,0:T(8,...) custom-call(f32[512,128]{1,0:T(8,128)S(1)} %bitcast.8, ...), custom_call_target="tpu_custom_call" | custom-call | flops 4194304 | bytes 4194304 | tf_op jit(solution)/shard_map/first/pallas_call | solution.py:592
  18.1 2.5 %collective-permute-start.7 = (f32[96,128]{1,0:T(8,128)S(1)}, f32[96,128]{1,0:T(8,128)S(1)}, u32[]{:S(2)}, u32[]{:S(2)}) collective-permute-start(f32[96,128]{1,0:T(8,128)S(1)} %get-tuple-element.37.refs_0_), channel_id=1, source_target_pairs={{0,3},{1,2},{2,1},{3,0},{4,7},{5,6},{6,5},{7,4},{8,11},{9,10},{10,... | collective-permute-start | bytes 147464 | tf_op jit(solution)/shard_map/ppermute | solution.py:631
  20.6 0.5 %collective-permute-start.6 = (f32[96,128]{1,0:T(8,128)S(1)}, f32[96,128]{1,0:T(8,128)S(1)}, u32[]{:S(2)}, u32[]{:S(2)}) collective-permute-start(f32[96,128]{1,0:T(8,128)S(1)} %get-tuple-element.37.refs_0_), channel_id=1, source_target_pairs={{0,2},{1,3},{2,0},{3,1},{4,6},{5,7},{6,4},{7,5},{8,10},{9,11},{10,... | collective-permute-start | bytes 147464 | tf_op jit(solution)/shard_map/ppermute | solution.py:631
  21.1 0.5 %collective-permute-start.5 = (f32[96,128]{1,0:T(8,128)S(1)}, f32[96,128]{1,0:T(8,128)S(1)}, u32[]{:S(2)}, u32[]{:S(2)}) collective-permute-start(f32[96,128]{1,0:T(8,128)S(1)} %get-tuple-element.37.refs_0_), channel_id=1, source_target_pairs={{0,1},{1,0},{2,3},{3,2},{4,5},{5,4},{6,7},{7,6},{8,9},{9,8},{10,11... | collective-permute-start | bytes 147464 | tf_op jit(solution)/shard_map/ppermute | solution.py:631
  21.6 1.6 %collective-permute-done.7.refs_3_ = f32[96,128]{1,0:T(8,128)S(1)} collective-permute-done((f32[96,128]{1,0:T(8,128)S(1)}, f32[96,128]{1,0:T(8,128)S(1)}, u32[]{:S(2)}, u32[]{:S(2)}) %collective-permute-start.7) | collective-permute-done | bytes 49184 | tf_op jit(solution)/shard_map/ppermute | solution.py:631
  23.2 1.5 %collective-permute-done.6.refs_2_ = f32[96,128]{1,0:T(8,128)S(1)} collective-permute-done((f32[96,128]{1,0:T(8,128)S(1)}, f32[96,128]{1,0:T(8,128)S(1)}, u32[]{:S(2)}, u32[]{:S(2)}) %collective-permute-start.6) | collective-permute-done | bytes 49184 | tf_op jit(solution)/shard_map/ppermute | solution.py:631
  24.7 0.5 %collective-permute-done.5.refs_1_ = f32[96,128]{1,0:T(8,128)S(1)} collective-permute-done((f32[96,128]{1,0:T(8,128)S(1)}, f32[96,128]{1,0:T(8,128)S(1)}, u32[]{:S(2)}, u32[]{:S(2)}) %collective-permute-start.5) | collective-permute-done | bytes 49184 | tf_op jit(solution)/shard_map/ppermute | solution.py:631
  25.2 3.9 %second.1 = (f32[96,128]{1,0:T(8,128)S(1)}, f32[512,128]{1,0:T(8,128)S(1)}, f32[512,128]{1,0:T(8,128)S(1)}, f32[512,128]{1,0:T(8,128)S(1)}, f32[512,128]{1,0:T(8,128)S(1)}) custom-call(f32[96,128]{1,0:T(8,128)S(1)} %get-tuple-element.37.refs_0_, f32[96,128]{1,0:T(8,128)S(1)} %collective-permute-done.5.refs_1_, f32[96,128]{1,0:T(8,128)S(1)} %collective-permute-done.6.refs_2_, ...), custom_call_target="tpu_custom_call" | custom-call | flops 4194304 | bytes 4194304 | tf_op jit(solution)/shard_map/second/pallas_call | solution.py:592
  29.1 1.6 %collective-permute-start.10 = (f32[96,128]{1,0:T(8,128)S(1)}, f32[96,128]{1,0:T(8,128)S(1)}, u32[]{:S(2)}, u32[]{:S(2)}) collective-permute-start(f32[96,128]{1,0:T(8,128)S(1)} %get-tuple-element.51.refs_0_), channel_id=1, source_target_pairs={{0,3},{1,2},{2,1},{3,0},{4,7},{5,6},{6,5},{7,4},{8,11},{9,10},{10,... | collective-permute-start | bytes 147464 | tf_op jit(solution)/shard_map/ppermute | solution.py:631
  30.7 0.6 %collective-permute-start.9 = (f32[96,128]{1,0:T(8,128)S(1)}, f32[96,128]{1,0:T(8,128)S(1)}, u32[]{:S(2)}, u32[]{:S(2)}) collective-permute-start(f32[96,128]{1,0:T(8,128)S(1)} %get-tuple-element.51.refs_0_), channel_id=1, source_target_pairs={{0,2},{1,3},{2,0},{3,1},{4,6},{5,7},{6,4},{7,5},{8,10},{9,11},{10,... | collective-permute-start | bytes 147464 | tf_op jit(solution)/shard_map/ppermute | solution.py:631
  31.2 1.4 %collective-permute-start.8 = (f32[96,128]{1,0:T(8,128)S(1)}, f32[96,128]{1,0:T(8,128)S(1)}, u32[]{:S(2)}, u32[]{:S(2)}) collective-permute-start(f32[96,128]{1,0:T(8,128)S(1)} %get-tuple-element.51.refs_0_), channel_id=1, source_target_pairs={{0,1},{1,0},{2,3},{3,2},{4,5},{5,4},{6,7},{7,6},{8,9},{9,8},{10,11... | collective-permute-start | bytes 147464 | tf_op jit(solution)/shard_map/ppermute | solution.py:631
  32.7 1.6 %collective-permute-done.10.refs_3_ = f32[96,128]{1,0:T(8,128)S(1)} collective-permute-done((f32[96,128]{1,0:T(8,128)S(1)}, f32[96,128]{1,0:T(8,128)S(1)}, u32[]{:S(2)}, u32[]{:S(2)}) %collective-permute-start.10) | collective-permute-done | bytes 49184 | tf_op jit(solution)/shard_map/ppermute | solution.py:631
  34.3 0.5 %collective-permute-done.9.refs_2_ = f32[96,128]{1,0:T(8,128)S(1)} collective-permute-done((f32[96,128]{1,0:T(8,128)S(1)}, f32[96,128]{1,0:T(8,128)S(1)}, u32[]{:S(2)}, u32[]{:S(2)}) %collective-permute-start.9) | collective-permute-done | bytes 49184 | tf_op jit(solution)/shard_map/ppermute | solution.py:631
  34.8 0.5 %collective-permute-done.8.refs_1_ = f32[96,128]{1,0:T(8,128)S(1)} collective-permute-done((f32[96,128]{1,0:T(8,128)S(1)}, f32[96,128]{1,0:T(8,128)S(1)}, u32[]{:S(2)}, u32[]{:S(2)}) %collective-permute-start.8) | collective-permute-done | bytes 49184 | tf_op jit(solution)/shard_map/ppermute | solution.py:631
  35.3 0.0 copy-done.2
  35.3 1.8 %last.1 = (f32[512,128]{1,0:T(8,128)}, f32[512,128]{1,0:T(8,128)}) custom-call(f32[96,128]{1,0:T(8,128)S(1)} %get-tuple-element.51.refs_0_, f32[96,128]{1,0:T(8,128)S(1)} %collective-permute-done.8.refs_1_, f32[96,128]{1,0:T(8,128)S(1)} %collective-permute-done.9.refs_2_, f32[96,128]{1,0:T(8,128)S(1)} %collective-permute-done.10.refs_3_, ...), custom_call_target="tpu_custom_call" | custom-call | flops 4194304 | bytes 4194304 | tf_op jit(solution)/shard_map/last/pallas_call | solution.py:592
  (5 shorter events, 0.0 us)
Async XLA Ops:
  0.6 0.7 %copy-start.4 = (s32[1,1,256]{2,1,0:T(1,128)S(1)}, s32[1,1,256]{2,1,0:T(1,128)}, u32[]{:S(2)}) copy-start(s32[1,1,256]{2,1,0:T(1,128)} %param.7) | copy-start | bytes 3076
  1.3 0.9 %copy-start = (f32[64,8,128]{2,1,0:T(8,128)S(1)}, f32[64,8,128]{2,1,0:T(8,128)}, u32[]{:S(2)}) copy-start(f32[64,8,128]{2,1,0:T(8,128)} %param.4) | copy-start | bytes 786436
  2.3 0.9 %copy-start.1 = (s32[64,8,128]{2,1,0:T(8,128)S(1)}, s32[64,8,128]{2,1,0:T(8,128)}, u32[]{:S(2)}) copy-start(s32[64,8,128]{2,1,0:T(8,128)} %param.6) | copy-start | bytes 786436
  3.2 0.9 %copy-start.3 = (f32[64,8,128]{2,1,0:T(8,128)S(1)}, f32[64,8,128]{2,1,0:T(8,128)}, u32[]{:S(2)}) copy-start(f32[64,8,128]{2,1,0:T(8,128)} %param.5) | copy-start | bytes 786436
  4.5 12.1 %collective-permute-start = (f32[392,128]{1,0:T(8,128)S(1)}, f32[392,128]{1,0:T(8,128)S(1)}, u32[]{:S(2)}, u32[]{:S(2)}) collective-permute-start(f32[392,128]{1,0:T(8,128)S(1)} %get-tuple-element.35), channel_id=1, source_target_pairs={{0,16},{16,0},{1,17},{17,1},{2,18},{18,2},{3,19},{19,3},{4,20},{20... | collective-permute-start | bytes 602120 | tf_op jit(solution)/shard_map/ppermute | solution.py:614
  5.0 6.1 %collective-permute-start.2 = (f32[72,128]{1,0:T(8,128)S(1)}, f32[72,128]{1,0:T(8,128)S(1)}, u32[]{:S(2)}, u32[]{:S(2)}) collective-permute-start(f32[72,128]{1,0:T(8,128)S(1)} %get-tuple-element.36.columns), channel_id=1, source_target_pairs={{4,8},{8,4},{5,9},{9,5},{6,10},{10,6},{7,11},{11,7},{20,24},{24,20... | collective-permute-start | bytes 110600 | tf_op jit(solution)/shard_map/ppermute | solution.py:613
  5.7 7.4 %collective-permute-start.1 = (f32[72,128]{1,0:T(8,128)S(1)}, f32[72,128]{1,0:T(8,128)S(1)}, u32[]{:S(2)}, u32[]{:S(2)}) collective-permute-start(f32[72,128]{1,0:T(8,128)S(1)} %get-tuple-element.36.columns), channel_id=1, source_target_pairs={{4,0},{0,4},{12,8},{8,12},{5,1},{1,5},{13,9},{9,13},{6,2},{2,6},{1... | collective-permute-start | bytes 110600 | tf_op jit(solution)/shard_map/ppermute | solution.py:612
  11.2 5.4 %collective-permute-start.4 = (f32[72,128]{1,0:T(8,128)S(1)}, f32[72,128]{1,0:T(8,128)S(1)}, u32[]{:S(2)}, u32[]{:S(2)}) collective-permute-start(f32[72,128]{1,0:T(8,128)S(1)} %collective-permute-done.2.from_odd), channel_id=1, source_target_pairs={{0,16},{16,0},{1,17},{17,1},{2,18},{18,2},{3,19},{19,3},{4,20},{20... | collective-permute-start | bytes 110600 | tf_op jit(solution)/shard_map/ppermute | solution.py:616
  13.1 3.5 %collective-permute-start.3 = (f32[72,128]{1,0:T(8,128)S(1)}, f32[72,128]{1,0:T(8,128)S(1)}, u32[]{:S(2)}, u32[]{:S(2)}) collective-permute-start(f32[72,128]{1,0:T(8,128)S(1)} %collective-permute-done.1.from_even), channel_id=1, source_target_pairs={{0,16},{16,0},{1,17},{17,1},{2,18},{18,2},{3,19},{19,3},{4,20},{20... | collective-permute-start | bytes 110600 | tf_op jit(solution)/shard_map/ppermute | solution.py:615
  18.1 5.1 %collective-permute-start.7 = (f32[96,128]{1,0:T(8,128)S(1)}, f32[96,128]{1,0:T(8,128)S(1)}, u32[]{:S(2)}, u32[]{:S(2)}) collective-permute-start(f32[96,128]{1,0:T(8,128)S(1)} %get-tuple-element.37.refs_0_), channel_id=1, source_target_pairs={{0,3},{1,2},{2,1},{3,0},{4,7},{5,6},{6,5},{7,4},{8,11},{9,10},{10,... | collective-permute-start | bytes 147464 | tf_op jit(solution)/shard_map/ppermute | solution.py:631
  20.6 4.1 %collective-permute-start.6 = (f32[96,128]{1,0:T(8,128)S(1)}, f32[96,128]{1,0:T(8,128)S(1)}, u32[]{:S(2)}, u32[]{:S(2)}) collective-permute-start(f32[96,128]{1,0:T(8,128)S(1)} %get-tuple-element.37.refs_0_), channel_id=1, source_target_pairs={{0,2},{1,3},{2,0},{3,1},{4,6},{5,7},{6,4},{7,5},{8,10},{9,11},{10,... | collective-permute-start | bytes 147464 | tf_op jit(solution)/shard_map/ppermute | solution.py:631
  21.1 4.1 %collective-permute-start.5 = (f32[96,128]{1,0:T(8,128)S(1)}, f32[96,128]{1,0:T(8,128)S(1)}, u32[]{:S(2)}, u32[]{:S(2)}) collective-permute-start(f32[96,128]{1,0:T(8,128)S(1)} %get-tuple-element.37.refs_0_), channel_id=1, source_target_pairs={{0,1},{1,0},{2,3},{3,2},{4,5},{5,4},{6,7},{7,6},{8,9},{9,8},{10,11... | collective-permute-start | bytes 147464 | tf_op jit(solution)/shard_map/ppermute | solution.py:631
  25.2 10.1 %copy-start.2 = (s32[64,8,128]{2,1,0:T(8,128)S(1)}, s32[64,8,128]{2,1,0:T(8,128)}, u32[]{:S(2)}) copy-start(s32[64,8,128]{2,1,0:T(8,128)} %param.6) | copy-start | bytes 786436
  29.1 5.2 %collective-permute-start.10 = (f32[96,128]{1,0:T(8,128)S(1)}, f32[96,128]{1,0:T(8,128)S(1)}, u32[]{:S(2)}, u32[]{:S(2)}) collective-permute-start(f32[96,128]{1,0:T(8,128)S(1)} %get-tuple-element.51.refs_0_), channel_id=1, source_target_pairs={{0,3},{1,2},{2,1},{3,0},{4,7},{5,6},{6,5},{7,4},{8,11},{9,10},{10,... | collective-permute-start | bytes 147464 | tf_op jit(solution)/shard_map/ppermute | solution.py:631
  30.7 4.2 %collective-permute-start.9 = (f32[96,128]{1,0:T(8,128)S(1)}, f32[96,128]{1,0:T(8,128)S(1)}, u32[]{:S(2)}, u32[]{:S(2)}) collective-permute-start(f32[96,128]{1,0:T(8,128)S(1)} %get-tuple-element.51.refs_0_), channel_id=1, source_target_pairs={{0,2},{1,3},{2,0},{3,1},{4,6},{5,7},{6,4},{7,5},{8,10},{9,11},{10,... | collective-permute-start | bytes 147464 | tf_op jit(solution)/shard_map/ppermute | solution.py:631
  31.2 4.1 %collective-permute-start.8 = (f32[96,128]{1,0:T(8,128)S(1)}, f32[96,128]{1,0:T(8,128)S(1)}, u32[]{:S(2)}, u32[]{:S(2)}) collective-permute-start(f32[96,128]{1,0:T(8,128)S(1)} %get-tuple-element.51.refs_0_), channel_id=1, source_target_pairs={{0,1},{1,0},{2,3},{3,2},{4,5},{5,4},{6,7},{7,6},{8,9},{9,8},{10,11... | collective-permute-start | bytes 147464 | tf_op jit(solution)/shard_map/ppermute | solution.py:631
